TPU v7x, 256 devices: a whole 4x4x8 slice. The times are simulated.
256 devices in a mesh: depth: 16 (over x_lo, z), tok: 16 (over x_hi, y, core).
Axes of the slice: x: 4 (x_hi: 2, x_lo: 2; x = x_hi * 2 + x_lo), y: 4, z: 8, core: 2. Of those that a mesh axis runs over, the one named last changes fastest.
Arguments:
- states: bfloat16 [16, 16384, 2048], P('depth', 'tok'), may hold values from -40 to 40
- w_query: bfloat16 [2048, 1024], replicated, may hold values from -0.25 to 0.25
- w_key: bfloat16 [2048, 256], replicated, may hold values from -0.25 to 0.25
- w_value: bfloat16 [2048, 256], replicated, may hold values from -0.125 to 0.125
Outputs:
- window_out: bfloat16 [16, 16384, 1024], P('depth', 'tok')
- depth_out: bfloat16 [16384, 1024], P(('tok', 'depth'))
All inputs are finite; a program needn't handle non-finite values.
Results may differ from a plain program's by a relative error of at most 0.012.
The roundings to bfloat16 on the way count: a program that leaves them out, or rounds other values in their place, can miss the bound.
Values may be sent and summed in bfloat16 or wider, within the bound.
A program may use at most 192 MiB of HBM per device.

v0:
```python
import jax
import jax.numpy as jnp
from jax import lax
from jax.sharding import PartitionSpec as P

HQ = 8
HK = 2
HD = 128
WINDOW = 256


def from_behind(value, axis, steps):
    count = lax.axis_size(axis)
    first, last = (max(0, -steps), min(count, count - steps))
    return lax.ppermute(value, axis, [(source, source + steps) for source in range(first, last)])


def in_one_piece(arrays, axis, split_dim, concat_dim, along):
    both = jnp.concatenate(arrays, axis=along)
    out, at, outs = (
        lax.all_to_all(both, axis, split_axis=split_dim, concat_axis=concat_dim, tiled=True),
        0,
        [],
    )
    for a in arrays:
        outs.append(lax.slice_in_dim(out, at, at + a.shape[along], axis=along))
        at += a.shape[along]
    return tuple(outs)


def project(rows, weight):
    return jnp.dot(rows, weight, preferred_element_type=jnp.float32).astype(jnp.bfloat16)


def band_attend(query, ext_key, ext_value, base):
    rows = query.shape[0]
    length = ext_key.shape[0]
    group = HQ // HK
    q_heads = query.reshape(rows, HK, group, HD)
    k_heads = ext_key.reshape(length, HK, HD)
    v_heads = ext_value.reshape(length, HK, HD)
    scores = jnp.einsum("qkgd,lkd->kgql", q_heads, k_heads, preferred_element_type=jnp.float32)
    scores = scores / jnp.sqrt(jnp.float32(HD))
    qpos = jnp.arange(rows, dtype=jnp.int32)[:, None]
    kidx = jnp.arange(length, dtype=jnp.int32)[None, :]
    allowed = (kidx >= qpos) & (kidx <= qpos + WINDOW) & (base - WINDOW + kidx >= 0)
    scores = jnp.where(allowed, scores, -jnp.inf)
    top = jnp.max(scores, axis=-1, keepdims=True)
    expo = jnp.exp(scores - top)
    weight = (expo / jnp.sum(expo, axis=-1, keepdims=True)).astype(jnp.bfloat16)
    out = jnp.einsum("kgql,lkd->qkgd", weight, v_heads, preferred_element_type=jnp.float32)
    return out.astype(jnp.bfloat16).reshape(rows, HQ * HD)


def depth_attend(final_q, keys, values):
    steps, count = (keys.shape[0], keys.shape[1])
    group = HQ // HK
    q_heads = final_q.reshape(count, HK, group, HD).astype(jnp.float32)
    k_steps = keys.reshape(steps, count, HK, HD).astype(jnp.float32)
    v_steps = values.reshape(steps, count, HK, HD).astype(jnp.float32)
    scores = jnp.einsum("tkgd,stkd->tkgs", q_heads, k_steps) / jnp.sqrt(jnp.float32(HD))
    top = jnp.max(scores, axis=-1, keepdims=True)
    expo = jnp.exp(scores - top)
    weight = expo / jnp.sum(expo, axis=-1, keepdims=True)
    out = jnp.einsum("tkgs,stkd->tkgd", weight, v_steps)
    return out.astype(jnp.bfloat16).reshape(count, HQ * HD)


def body(states, w_query, w_key, w_value):
    local = states[0]
    rows = local.shape[0]
    steps = lax.axis_size("depth")
    shard = lax.axis_index("tok")
    query = project(local, w_query)
    key = project(local, w_key)
    value = project(local, w_value)
    rim_key, rim_value = from_behind((key[rows - WINDOW :], value[rows - WINDOW :]), "tok", 1)
    ext_key = jnp.concatenate([rim_key, key], axis=0)
    ext_value = jnp.concatenate([rim_value, value], axis=0)
    window_out = band_attend(query, ext_key, ext_value, shard * rows)[None]
    keys, values, queries = in_one_piece((key[None], value[None], query[None]), "depth", 1, 0, 2)
    final_q = queries[steps - 1]
    depth_out = depth_attend(final_q, keys, values)
    return (window_out, depth_out)


def solution(mesh):
    in_specs = (P("depth", "tok", None), P(), P(), P())
    out_specs = (P("depth", "tok", None), P(("tok", "depth"), None))
    return jax.shard_map(body, mesh=mesh, in_specs=in_specs, out_specs=out_specs, check_vma=False)
```

profile of v0, /device:TPU:56, one launch (start us, length us, event | category | flops | bytes accessed | tf_op | source)
XLA Modules:
  0.0 165.4 jit_solution(13551005565695763357)
XLA Ops:
  0.6 0.0 copy-start
  0.6 0.0 copy-start.3
  0.7 1.2 copy-done
  1.9 3.4 %fusion.18 = bf16[1024,256]{1,0:T(8,128)(2,1)S(1)} fusion(bf16[2048,256]{1,0:T(8,128)(2,1)S(1)} %copy-done, bf16[1,1024,2048]{2,1,0:T(8,128)(2,1)} %param.4), kind=kOutput, calls=%fused_computation.20 | convolution fusion | flops 1074003968 | bytes 5767168 | tf_op jit(solution)/shard_map/dot_general | solution.py:32
  5.3 0.2 copy.28
  5.5 0.0 copy-done.3
  5.5 3.4 %fusion.15 = bf16[1024,256]{1,0:T(8,128)(2,1)S(1)} fusion(bf16[2048,256]{1,0:T(8,128)(2,1)S(1)} %copy-done.3, bf16[1,1024,2048]{2,1,0:T(8,128)(2,1)} %param.4), kind=kOutput, calls=%fused_computation.19 | convolution fusion | flops 1074003968 | bytes 5767168 | tf_op jit(solution)/shard_map/dot_general | solution.py:32
  9.0 0.2 copy.29
  9.2 8.0 %fusion.12 = bf16[1024,1024]{0,1:T(8,128)(2,1)S(1)} fusion(bf16[2048,1024]{1,0:T(8,128)(2,1)} %param.5, bf16[1,1024,2048]{2,1,0:T(8,128)(2,1)} %param.4), kind=kOutput, calls=%fused_computation.18 | convolution fusion | flops 4296015872 | bytes 10485760 | tf_op jit(solution)/shard_map/dot_general | solution.py:32
  17.2 0.0 copy-start.2
  17.2 1.3 copy-done.2
  18.5 2.0 %pad_maximum_fusion = bf16[1,1024,1536]{1,2,0:T(8,128)(2,1)} fusion(bf16[1,1024,1024]{1,2,0:T(8,128)(2,1)S(1)} %bitcast.49, bf16[1,1024,256]{1,2,0:T(8,128)(2,1)S(1)} %copy.29, bf16[1,1024,256]{1,2,0:T(8,128)(2,1)S(1)} %copy.28), kind=kLoop, calls=%fused_computation.16 | loop fusion | flops 9437184 | bytes 6291456 | tf_op jit(solution)/shard_map/concatenate | solution.py:19
  20.5 15.8 %copy.30 = bf16[1,1024,1536]{2,0,1:T(2,128)(2,1)} copy(bf16[1,1024,1536]{1,2,0:T(8,128)(2,1)} %pad_maximum_fusion) | data formatting | bytes 6291456 | tf_op jit(solution)/shard_map/concatenate | solution.py:19
  36.3 0.5 broadcast.23
  36.9 22.0 %reduce = bf16[1024,1536]{1,0:T(8,128)(2,1)} reduce(bf16[1024,1,1536]{2,1,0:T(2,128)(2,1)} %bitcast.43, bf16[]{:T(256)} %broadcast.23), dimensions={1}, to_apply=%bitcast.33.reduce_sub_computation | reduce | bytes 6291458
  58.9 7.1 %reshape.49 = bf16[16,2,49152]{2,1,0:T(2,128)(2,1)} reshape(bf16[1024,1536]{1,0:T(8,128)(2,1)} %reduce) | data formatting | bytes 6291456
  66.0 9.5 %all-to-all-start = ((bf16[16,2,49152]{2,1,0:T(2,128)(2,1)}), bf16[16,2,49152]{2,1,0:T(2,128)(2,1)}, u32[]{:S(2)}, u32[]{:S(2)}) async-start(bf16[16,2,49152]{2,1,0:T(2,128)(2,1)} %reshape.49), calls=%async_computation | async-start | bytes 6291456 | tf_op jit(solution)/shard_map/all_to_all | solution.py:21
  75.5 1.9 %collective-permute-start.1 = (bf16[256,256]{1,0:T(8,128)(2,1)S(1)}, bf16[256,256]{1,0:T(8,128)(2,1)S(1)}, u32[]{:S(2)}, u32[]{:S(2)}) collective-permute-start(bf16[256,256]{1,0:T(8,128)(2,1)S(1)} %slice.23), channel_id=1, source_target_pairs={{0,1},{1,2},{2,3},{3,4},{4,5},{5,6},{6,7},{7,8},{8,9},{9,10},{10,1... | collective-permute-start | bytes 393224 | tf_op jit(solution)/shard_map/ppermute | solution.py:15
  77.4 4.6 %collective-permute-start = (bf16[256,256]{1,0:T(8,128)(2,1)S(1)}, bf16[256,256]{1,0:T(8,128)(2,1)S(1)}, u32[]{:S(2)}, u32[]{:S(2)}) collective-permute-start(bf16[256,256]{1,0:T(8,128)(2,1)S(1)} %slice.22), channel_id=1, source_target_pairs={{0,1},{1,2},{2,3},{3,4},{4,5},{5,6},{6,7},{7,8},{8,9},{9,10},{10,1... | collective-permute-start | bytes 393224 | tf_op jit(solution)/shard_map/ppermute | solution.py:15
  82.0 1.8 %fusion.4 = pred[1024,1280]{0,1:T(8,128)(4,1)S(1)} fusion(s32[1024]{0:T(1024)S(1)} %iota_add_fusion, pred[1280]{0:T(1024)(128)(4,1)S(1)} %add_compare_fusion), kind=kLoop, calls=%fused_computation.9 | loop fusion | flops 5242880 | bytes 1316096 | tf_op jit(solution)/shard_map/and | solution.py:46
  83.8 0.0 collective-permute-done.1
  83.9 1.0 reshape.42
  84.9 0.0 collective-permute-done
  85.0 0.2 copy.38
  85.2 19.9 %exponential_reduce_fusion = (f32[2,4,1024]{2,1,0:T(4,128)S(1)}, f32[2,4,1024,1280]{2,3,1,0:T(8,128)}) fusion(bf16[1024,2,4,128]{0,3,2,1:T(8,128)(2,1)} %bitcast.50, pred[1024,1280]{0,1:T(8,128)(4,1)S(1)} %fusion.4, bf16[1280,2,128,1]{2,1,0,3:T(2,128)(2,1)} %bitcast.52), kind=kOutput, calls=%fused_computation.4 | convolution fusion | flops 2726298880 | bytes 46039040 | tf_op jit(solution)/shard_map/sub | solution.py:49
  105.1 16.6 %fusion.11 = bf16[2,128,4,1024]{3,1,2,0:T(8,128)(2,1)S(1)} fusion(bf16[1280,2,128,1]{0,2,3,1:T(8,128)(2,1)S(1)} %bitcast.53, f32[2,4,1024,1280]{2,3,1,0:T(8,128)} %get-tuple-element.11, f32[2,4,1024]{2,1,0:T(4,128)S(1)} %get-tuple-element.10), kind=kOutput, calls=%fused_computation.17 | convolution fusion | flops 2706374656 | bytes 44728320 | tf_op jit(solution)/shard_map/kgql,lkd->qkgd/dot_general | solution.py:51
  121.8 2.6 %copy.33 = bf16[1,1024,1024]{2,1,0:T(8,128)(2,1)} copy(bf16[1,1024,1024]{1,2,0:T(8,128)(2,1)S(1)} %bitcast.51) | data formatting | bytes 4194304
  124.3 23.1 %all-to-all-done = bf16[16,2,49152]{2,1,0:T(2,128)(2,1)} async-done(((bf16[16,2,49152]{2,1,0:T(2,128)(2,1)}), bf16[16,2,49152]{2,1,0:T(2,128)(2,1)}, u32[]{:S(2)}, u32[]{:S(2)}) %all-to-all-start) | async-done | bytes 3145760 | tf_op jit(solution)/shard_map/all_to_all | solution.py:21
  147.4 11.5 %reshape.50 = bf16[1024,1,1536]{2,1,0:T(2,128)(2,1)} reshape(bf16[16,2,49152]{2,1,0:T(2,128)(2,1)} %all-to-all-done) | data formatting | bytes 6291456
  158.9 3.6 %copy.41 = bf16[1,1024,1536]{2,1,0:T(8,128)(2,1)S(1)} copy(bf16[1,1024,1536]{2,0,1:T(2,128)(2,1)} %bitcast.44) | data formatting | bytes 6291456
  162.5 0.1 fusion.35
  162.7 0.1 reshape.44
  162.8 0.1 reshape_squeeze.3
  162.9 0.1 reshape.45
  163.0 0.6 fusion.38
  163.6 0.0 copy-start.1
  163.6 0.4 fusion.30
  164.0 0.6 convolution_convert_fusion
  164.6 0.7 reshape.46
  165.4 0.0 copy-done.1
  (7 shorter events, 0.1 us)
Async XLA Ops:
  0.6 1.2 copy-start
  0.6 4.9 %copy-start.3 = (bf16[2048,256]{1,0:T(8,128)(2,1)S(1)}, bf16[2048,256]{1,0:T(8,128)(2,1)}, u32[]{:S(2)}) copy-start(bf16[2048,256]{1,0:T(8,128)(2,1)} %param.7) | copy-start | bytes 3145732
  17.2 1.3 copy-start.2
  66.0 81.5 %all-to-all-start = ((bf16[16,2,49152]{2,1,0:T(2,128)(2,1)}), bf16[16,2,49152]{2,1,0:T(2,128)(2,1)}, u32[]{:S(2)}, u32[]{:S(2)}) async-start(bf16[16,2,49152]{2,1,0:T(2,128)(2,1)} %reshape.49), calls=%async_computation | async-start | bytes 6291456 | tf_op jit(solution)/shard_map/all_to_all | solution.py:21
  75.5 8.4 %collective-permute-start.1 = (bf16[256,256]{1,0:T(8,128)(2,1)S(1)}, bf16[256,256]{1,0:T(8,128)(2,1)S(1)}, u32[]{:S(2)}, u32[]{:S(2)}) collective-permute-start(bf16[256,256]{1,0:T(8,128)(2,1)S(1)} %slice.23), channel_id=1, source_target_pairs={{0,1},{1,2},{2,3},{3,4},{4,5},{5,6},{6,7},{7,8},{8,9},{9,10},{10,1... | collective-permute-start | bytes 393224 | tf_op jit(solution)/shard_map/ppermute | solution.py:15
  77.4 7.5 %collective-permute-start = (bf16[256,256]{1,0:T(8,128)(2,1)S(1)}, bf16[256,256]{1,0:T(8,128)(2,1)S(1)}, u32[]{:S(2)}, u32[]{:S(2)}) collective-permute-start(bf16[256,256]{1,0:T(8,128)(2,1)S(1)} %slice.22), channel_id=1, source_target_pairs={{0,1},{1,2},{2,3},{3,4},{4,5},{5,6},{6,7},{7,8},{8,9},{9,10},{10,1... | collective-permute-start | bytes 393224 | tf_op jit(solution)/shard_map/ppermute | solution.py:15
  163.6 1.7 %copy-start.1 = (bf16[2048,256]{1,0:T(8,128)(2,1)S(1)}, bf16[2048,256]{1,0:T(8,128)(2,1)}, u32[]{:S(2)}) copy-start(bf16[2048,256]{1,0:T(8,128)(2,1)} %param.6) | copy-start | bytes 3145732
where the time goes:
time: 167 us; the launch traced here: 165 us
  matrix products  52.6 us (31%)
  local copies, waits for them, and re-layouts  46.4 us (28%)
  other arithmetic  26.3 us (16%)
  waiting for transfers between devices  23.1 us (14%)
  starting transfers between devices  16 us (10%)
    unnamed x13, local copies, waits for them, and re-layouts  27.8 us
    all_to_all x1, waiting for transfers between devices, in_one_piece(): lax.all_to_all(both, axis, split_axis=split_dim, concat_axis=concat_dim,...  23.1 us
    unnamed x1, other arithmetic  22 us
    sub x1, matrix products, band_attend(): expo = jnp.exp(scores - top)  19.9 us
    dot_general x1, matrix products, band_attend(): jnp.einsum('kgql,lkd->qkgd', weight, v_heads, preferred_element_type=jnp....  16.6 us
    concatenate x1, local copies, waits for them, and re-layouts, in_one_piece(): both = jnp.concatenate(arrays, axis=along)  15.8 us
    dot_general x3, matrix products, project(): jnp.dot(rows, weight, preferred_element_type=jnp.float32)  14.9 us
    all_to_all x1, starting transfers between devices, in_one_piece(): lax.all_to_all(both, axis, split_axis=split_dim, concat_axis=concat_dim,...  9.51 us
  transfers between devices with their start and end apart: 3, of which 1 were waited for; matrix products, arithmetic and copies ran while one was open for 26% of the time, Pallas kernels for 0%

commit v1 on v0

v1 whole, which is shorter than its diff:
```python
import math

import jax
import jax.numpy as jnp
from jax import lax
from jax.experimental import pallas as pl
from jax.experimental.pallas import tpu as pltpu
from jax.sharding import PartitionSpec as P

HQ = 8
HK = 2
HD = 128
GROUP = HQ // HK
WINDOW = 256
D = 2048
QW = HQ * HD
KW = HK * HD
TOK = 1024
STEPS = 16
OWN = TOK // STEPS
CHUNK = 256
BQ = 128
KEYS = BQ + WINDOW
RELAY = 7
LAST = STEPS - 1
SCALE = math.log2(math.e) / math.sqrt(HD)
MESH = pl.DeviceIdType.MESH
F32 = jnp.float32
BF16 = jnp.bfloat16


def softmax_values(scores, values):
    top = jnp.max(scores, axis=-1, keepdims=True)
    weight = jnp.exp2((scores - top) * SCALE).astype(BF16)
    ext = jnp.concatenate([values, jnp.ones_like(values)], axis=1)
    out = jnp.dot(weight, ext, preferred_element_type=F32)
    return out[:, :HD] / out[:, HD:]


def score(rows, keys):
    return lax.dot_general(rows, keys, (((1,), (1,)), ((), ())), preferred_element_type=F32)


def kernel(
    x_hbm, wq_hbm, wk_hbm, wv_hbm, win_hbm, dep_hbm,
    x, wq, wkv, q, kv, kvr, qr, relay, out, dout, bias,
    ld, st, ss, rs, qs_sem, qr_sem, rel_sem, halo_s, halo_r,
):
    me = lax.axis_index("depth")
    shard = lax.axis_index("tok")
    shards = lax.axis_size("tok")
    x_lo = me // 8
    z_hi = (me // 4) % 2
    has_next = shard < shards - 1
    has_prev = shard > 0

    def chunk_of(i):
        return 2 * ((x_lo + 1 - i % 2) % 2) + (z_hi + 1 - i // 2) % 2

    def chunk_rows(i):
        return pl.ds(pl.multiple_of(chunk_of(i) * CHUNK, CHUNK), CHUNK)

    def load_x(i):
        rows = chunk_rows(i)
        return pltpu.make_async_copy(x_hbm.at[rows], x.at[rows], ld.at[i])

    load_k = pltpu.make_async_copy(wk_hbm, wkv.at[:, :KW], ld.at[4])
    load_v = pltpu.make_async_copy(wv_hbm, wkv.at[:, KW:], ld.at[5])
    load_q = pltpu.make_async_copy(wq_hbm, wq, ld.at[6])
    load_k.start()
    load_v.start()
    for i in range(4):
        load_x(i).start()
    load_q.start()

    barrier = pltpu.get_barrier_semaphore()
    for step in range(1, STEPS):
        pl.semaphore_signal(
            barrier, inc=1, device_id={"depth": lax.rem(me + step, STEPS)}, device_id_type=MESH
        )

    @pl.when(has_next)
    def _():
        pl.semaphore_signal(barrier, inc=1, device_id={"tok": shard + 1}, device_id_type=MESH)

    @pl.when(has_prev)
    def _():
        pl.semaphore_signal(barrier, inc=1, device_id={"tok": shard - 1}, device_id_type=MESH)

    row = lax.broadcasted_iota(jnp.int32, (BQ, KEYS), 0)
    col = lax.broadcasted_iota(jnp.int32, (BQ, KEYS), 1)
    band = (col >= row) & (col <= row + WINDOW)
    bias[0] = jnp.where(band, 0.0, -jnp.inf).astype(F32)
    for b in range(2):
        known = col + (b * BQ - WINDOW) + shard * TOK >= 0
        bias[1 + b] = jnp.where(band & known, 0.0, -jnp.inf).astype(F32)

    @pl.when(shard == 0)
    def _():
        kv[:WINDOW] = jnp.zeros((WINDOW, 2 * KW), BF16)

    load_k.wait()
    load_v.wait()

    def project_kv(i, carry):
        load_x(i).wait()
        rows = chunk_rows(i)
        kv[pl.ds(pl.multiple_of(WINDOW + chunk_of(i) * CHUNK, CHUNK), CHUNK)] = jnp.dot(
            x[rows], wkv[...], preferred_element_type=F32
        ).astype(BF16)
        return carry

    lax.fori_loop(0, 4, project_kv, 0)

    pl.semaphore_wait(
        barrier, STEPS - 1 + has_next.astype(jnp.int32) + has_prev.astype(jnp.int32)
    )

    def kv_copy(dest, source):
        rows = pl.ds(pl.multiple_of(WINDOW + dest * OWN, OWN), OWN)
        return pltpu.make_async_remote_copy(
            kv.at[rows], kvr.at[source], ss.at[dest], rs.at[source],
            device_id={"depth": dest}, device_id_type=MESH,
        )

    def send_kv(i):
        for j in range(4):
            dest = chunk_of(i) * 4 + j

            @pl.when(dest != me)
            def _():
                kv_copy(dest, me).start()

    halo = pltpu.make_async_remote_copy(
        kv.at[pl.ds(TOK, WINDOW)], kv.at[pl.ds(0, WINDOW)], halo_s, halo_r,
        device_id={"tok": lax.rem(shard + 1, shards)}, device_id_type=MESH,
    )

    def project_q(i):
        rows = pl.ds(pl.multiple_of(i * CHUNK, CHUNK), CHUNK)
        for n in range(2):
            cols = slice(n * 512, (n + 1) * 512)
            q[rows, cols] = jnp.dot(x[rows], wq[:, cols], preferred_element_type=F32).astype(BF16)

    def q_direct(dest):
        return pltpu.make_async_remote_copy(
            q.at[pl.ds(pl.multiple_of(dest * OWN, OWN), OWN)], qr, qs_sem.at[dest], qr_sem,
            device_id={"depth": dest}, device_id_type=MESH,
        )

    def q_to_relay(dest):
        return pltpu.make_async_remote_copy(
            q.at[pl.ds(pl.multiple_of(dest * OWN, OWN), OWN)], relay.at[dest],
            qs_sem.at[dest], rel_sem.at[dest],
            device_id={"depth": RELAY}, device_id_type=MESH,
        )

    def q_from_relay(dest):
        return pltpu.make_async_remote_copy(
            relay.at[dest], qr, qs_sem.at[dest], qr_sem,
            device_id={"depth": dest}, device_id_type=MESH,
        )

    for i in range(3):
        send_kv(i)
    load_q.wait()
    project_q(0)
    send_kv(3)

    @pl.when(has_next)
    def _():
        halo.start()

    project_q(1)

    @pl.when(me == LAST)
    def _():
        for j in range(4):
            q_to_relay(j).start()

    project_q(2)

    @pl.when(me == LAST)
    def _():
        for j in range(4, RELAY):
            q_to_relay(j).start()
        q_direct(RELAY).start()

    project_q(3)

    @pl.when(me == LAST)
    def _():
        for j in range(8, 12):
            q_direct(j).start()

    kvr[me] = kv[pl.ds(pl.multiple_of(WINDOW + me * OWN, OWN), OWN)]

    @pl.when(me == LAST)
    def _():
        qr[...] = q[pl.ds(LAST * OWN, OWN)]

    def attend(b, edge):
        base = pl.multiple_of(b * BQ, BQ)
        for c in range(HK):
            heads = [
                q[pl.ds(base, BQ), h * HD : (h + 1) * HD] for h in range(c * GROUP, (c + 1) * GROUP)
            ]
            rows = jnp.concatenate(heads, axis=0)
            keys = kv[pl.ds(base, KEYS), c * HD : (c + 1) * HD]
            values = kv[pl.ds(base, KEYS), KW + c * HD : KW + (c + 1) * HD]
            scores = score(rows, keys).reshape(GROUP, BQ, KEYS)
            if edge:
                scores = scores + bias[1 + b][None]
            else:
                scores = jnp.concatenate(
                    [
                        scores[:, :, :BQ] + bias[0, :, :BQ][None],
                        scores[:, :, BQ:WINDOW],
                        scores[:, :, WINDOW:] + bias[0, :, WINDOW:][None],
                    ],
                    axis=-1,
                )
            res = softmax_values(scores.reshape(GROUP * BQ, KEYS), values).astype(BF16)
            for g in range(GROUP):
                h = c * GROUP + g
                out[pl.ds(base, BQ), h * HD : (h + 1) * HD] = res[g * BQ : (g + 1) * BQ]

    def store(b):
        rows = pl.ds(pl.multiple_of(b * BQ, BQ), BQ)
        return pltpu.make_async_copy(out.at[rows], win_hbm.at[rows], st.at[b])

    def forward(i):
        @pl.when(me == RELAY)
        def _():
            q_to_relay(i).wait_recv()
            q_from_relay(i).start()

    def block(i, carry):
        attend(i + 2, False)

        @pl.when(i > 0)
        def _():
            store(i + 1).start()

        @pl.when((me == LAST) & (i == 0))
        def _():
            for j in range(12, LAST):
                q_direct(j).start()

        forward(i)
        return carry

    lax.fori_loop(0, 6, block, 0)
    forward(6)

    @pl.when(has_prev)
    def _():
        halo.wait_recv()

    attend(0, True)
    store(7).start()
    attend(1, True)
    store(0).start()

    for source in range(STEPS):

        @pl.when(me != source)
        def _():
            kv_copy(source, source).wait_recv()

    @pl.when(me != LAST)
    def _():
        q_direct(LAST).wait_recv()

    store(1).start()
    token = lax.broadcasted_iota(jnp.int32, (OWN, STEPS * OWN), 0)
    other = lax.broadcasted_iota(jnp.int32, (OWN, STEPS * OWN), 1) % OWN
    for c in range(HK):
        rows = jnp.concatenate(
            [qr[:, h * HD : (h + 1) * HD] for h in range(c * GROUP, (c + 1) * GROUP)], axis=0
        )
        keys = kvr[:, :, c * HD : (c + 1) * HD].reshape(STEPS * OWN, HD)
        values = kvr[:, :, KW + c * HD : KW + (c + 1) * HD].reshape(STEPS * OWN, HD)
        scores = score(rows, keys).reshape(GROUP, OWN, STEPS * OWN)
        scores = jnp.where((token == other)[None], scores, -jnp.inf)
        res = softmax_values(scores.reshape(GROUP * OWN, STEPS * OWN), values).astype(BF16)
        for g in range(GROUP):
            h = c * GROUP + g
            dout[:, h * HD : (h + 1) * HD] = res[g * OWN : (g + 1) * OWN]

    last = pltpu.make_async_copy(dout, dep_hbm, ld.at[0])
    last.start()
    for dest in range(STEPS):

        @pl.when(me != dest)
        def _():
            kv_copy(dest, dest).wait_send()

    @pl.when(has_next)
    def _():
        halo.wait_send()

    @pl.when(me == LAST)
    def _():
        for dest in range(LAST):
            q_direct(dest).wait_send()

    @pl.when(me == RELAY)
    def _():
        for dest in range(RELAY):
            q_from_relay(dest).wait_send()

    for b in range(TOK // BQ):
        store(b).wait()
    last.wait()


def body(states, w_query, w_key, w_value):
    any_spec = pl.BlockSpec(memory_space=pl.ANY)
    dma = pltpu.SemaphoreType.DMA
    window_out, depth_out = pl.pallas_call(
        kernel,
        out_shape=(
            jax.ShapeDtypeStruct((TOK, QW), BF16),
            jax.ShapeDtypeStruct((OWN, QW), BF16),
        ),
        in_specs=[any_spec] * 4,
        out_specs=(any_spec, any_spec),
        scratch_shapes=[
            pltpu.VMEM((TOK, D), BF16),
            pltpu.VMEM((D, QW), BF16),
            pltpu.VMEM((D, 2 * KW), BF16),
            pltpu.VMEM((TOK, QW), BF16),
            pltpu.VMEM((WINDOW + TOK, 2 * KW), BF16),
            pltpu.VMEM((STEPS, OWN, 2 * KW), BF16),
            pltpu.VMEM((OWN, QW), BF16),
            pltpu.VMEM((RELAY, OWN, QW), BF16),
            pltpu.VMEM((TOK, QW), BF16),
            pltpu.VMEM((OWN, QW), BF16),
            pltpu.VMEM((3, BQ, KEYS), F32),
            dma((7,)),
            dma((TOK // BQ,)),
            dma((STEPS,)),
            dma((STEPS,)),
            dma((STEPS,)),
            dma(()),
            dma((RELAY,)),
            dma(()),
            dma(()),
        ],
        compiler_params=pltpu.CompilerParams(
            collective_id=0, has_side_effects=True, vmem_limit_bytes=60 * 1024 * 1024
        ),
        name="looped_attention",
    )(states[0], w_query, w_key, w_value)
    return (window_out[None], depth_out)


def solution(mesh):
    in_specs = (P("depth", "tok", None), P(), P(), P())
    out_specs = (P("depth", "tok", None), P(("tok", "depth"), None))
    return jax.shard_map(body, mesh=mesh, in_specs=in_specs, out_specs=out_specs, check_vma=False)
```

time: 167 us -> 52.2 us (0.31)
  the two profiles are of different devices: /device:TPU:56 before, /device:TPU:217 now
where the time goes in v1:
time: 52.2 us; the launch traced here: 52.1 us
  Pallas kernels  47.7 us (91%)
  local copies, waits for them, and re-layouts  3.77 us (7%)
  between operations  0.65 us (1%)
    pallas_call x1, Pallas kernels, body(): pl.pallas_call(kernel, out_shape=(jax.ShapeDtypeStruct((TOK, QW), BF16),...  47.7 us
    unnamed x4, local copies, waits for them, and re-layouts  3.77 us

profile of v1, /device:TPU:217, one launch (start us, length us, event | category | flops | bytes accessed | tf_op | source)
XLA Modules:
  0.0 52.1 jit_solution(11196749449524345010)
XLA Ops:
  0.6 47.7 %looped_attention.1 = (bf16[1024,1024]{1,0:T(8,128)(2,1)}, bf16[64,1024]{1,0:T(8,128)(2,1)}) custom-call(bf16[1024,2048]{1,0:T(8,128)(2,1)} %bitcast.2, bf16[2048,1024]{1,0:T(8,128)(2,1)} %wq_hbm.1, bf16[2048,256]{1,0:T(8,128)(2,1)} %wk_hbm.1, bf16[2048,256]{1,0:T(8,128)(2,1)} %wv_hbm.1), custom_call_target="tpu_custom_call" | custom-call | tf_op jit(solution)/shard_map/looped_attention/pallas_call | solution.py:321
  48.3 0.0 copy-start
  48.3 3.1 %copy.8 = bf16[1,1024,1024]{2,1,0:T(8,128)(2,1)} copy(bf16[1,1024,1024]{2,1,0:T(8,128)(2,1)} %bitcast.3) | data formatting | bytes 4194304
  51.4 0.0 copy-done
  51.5 0.7 %copy.9 = bf16[64,1024]{1,0:T(8,128)(2,1)} copy(bf16[64,1024]{1,0:T(8,128)(2,1)S(1)} %copy-done) | data formatting | bytes 262144
Async XLA Ops:
  48.3 3.1 %copy-start = (bf16[64,1024]{1,0:T(8,128)(2,1)S(1)}, bf16[64,1024]{1,0:T(8,128)(2,1)}, u32[]{:S(2)}) copy-start(bf16[64,1024]{1,0:T(8,128)(2,1)} %get-tuple-element.9) | copy-start | bytes 393220

commit v2 on v1

v2 whole, which is shorter than its diff:
```python
import math

import jax
import jax.numpy as jnp
from jax import lax
from jax.experimental import pallas as pl
from jax.experimental.pallas import tpu as pltpu
from jax.sharding import PartitionSpec as P

HQ = 8
HK = 2
HD = 128
GROUP = HQ // HK
WINDOW = 256
D = 2048
QW = HQ * HD
KW = HK * HD
TOK = 1024
STEPS = 16
OWN = TOK // STEPS
CHUNK = 256
BQ = 128
KEYS = BQ + WINDOW
RELAY = 7
RELAYED = (3, 2, 4, 1, 5, 6)
DIRECT0 = (0, 7)
LAST = STEPS - 1
SCALE = math.log2(math.e) / math.sqrt(HD)
MESH = pl.DeviceIdType.MESH
F32 = jnp.float32
BF16 = jnp.bfloat16


def softmax_values(scores, values):
    top = jnp.max(scores, axis=-1, keepdims=True)
    weight = jnp.exp2((scores - top) * SCALE).astype(BF16)
    ext = jnp.concatenate([values, jnp.ones_like(values)], axis=1)
    out = jnp.dot(weight, ext, preferred_element_type=F32)
    return out[:, :HD] / out[:, HD:]


def score(rows, keys):
    return lax.dot_general(rows, keys, (((1,), (1,)), ((), ())), preferred_element_type=F32)


def kernel(
    x_hbm, wq_hbm, wk_hbm, wv_hbm, out, kvr, qr,
    x, wq, wkv, q, kv, relay, legs, bias,
    ld, ss, rs, legs_s, legs_r, qs_sem, qr_sem, rel_sem, halo_s, halo_r,
):
    me = lax.axis_index("depth")
    shard = lax.axis_index("tok")
    shards = lax.axis_size("tok")
    x_lo = me // 8
    z_hi = (me // 4) % 2
    has_next = shard < shards - 1
    has_prev = shard > 0

    def chunk_of(i):
        return 2 * ((x_lo + 1 - i % 2) % 2) + (z_hi + 1 - i // 2) % 2

    def chunk_rows(i):
        return pl.ds(pl.multiple_of(chunk_of(i) * CHUNK, CHUNK), CHUNK)

    def load_x(i):
        rows = chunk_rows(i)
        return pltpu.make_async_copy(x_hbm.at[rows], x.at[rows], ld.at[i])

    load_k = pltpu.make_async_copy(wk_hbm, wkv.at[:, :KW], ld.at[4])
    load_v = pltpu.make_async_copy(wv_hbm, wkv.at[:, KW:], ld.at[5])
    load_q = pltpu.make_async_copy(wq_hbm, wq, ld.at[6])
    is_last = me == LAST

    @pl.when(is_last)
    def _():
        load_k.start()
        load_v.start()
        for i in (3, 0, 2, 1):
            load_x(i).start()
        load_q.start()

    @pl.when(me != LAST)
    def _():
        load_k.start()
        load_v.start()
        for i in range(4):
            load_x(i).start()

    barrier = pltpu.get_barrier_semaphore()
    for step in range(1, STEPS):
        pl.semaphore_signal(
            barrier, inc=1, device_id={"depth": lax.rem(me + step, STEPS)}, device_id_type=MESH
        )

    @pl.when(has_next)
    def _():
        pl.semaphore_signal(barrier, inc=1, device_id={"tok": shard + 1}, device_id_type=MESH)

    @pl.when(has_prev)
    def _():
        pl.semaphore_signal(barrier, inc=1, device_id={"tok": shard - 1}, device_id_type=MESH)

    @pl.when(shard == 0)
    def _():
        kv[:WINDOW] = jnp.zeros((WINDOW, 2 * KW), BF16)

    def project_kv(i, carry):
        kv[pl.ds(pl.multiple_of(WINDOW + chunk_of(i) * CHUNK, CHUNK), CHUNK)] = jnp.dot(
            x[chunk_rows(i)], wkv[...], preferred_element_type=F32
        ).astype(BF16)
        return carry

    def project_q(i):
        rows = pl.ds(pl.multiple_of(i * CHUNK, CHUNK), CHUNK)
        for n in range(2):
            cols = slice(n * 512, (n + 1) * 512)
            q[rows, cols] = jnp.dot(x[rows], wq[:, cols], preferred_element_type=F32).astype(BF16)

    def project_q_loop(i, carry):
        project_q(i)
        return carry

    def own_rows(dest):
        return pl.ds(pl.multiple_of(WINDOW + dest * OWN, OWN), OWN)

    def kv_copy(dest, source):
        return pltpu.make_async_remote_copy(
            kv.at[own_rows(dest)], kvr.at[source], ss.at[dest], rs.at[source],
            device_id={"depth": dest}, device_id_type=MESH,
        )

    z = me % 8
    detour = (z == 1) | (z == 4)
    detour_to = jnp.where(z == 1, 5, 0)
    via = x_lo * 8 + jnp.where(z == 1, 3, 2)
    between = (z == 3) | (z == 2)
    between_src = x_lo * 8 + jnp.where(z == 3, 1, 4)
    between_dst = jnp.where(z == 3, 5, 0)

    def first_leg(slot):
        return pltpu.make_async_remote_copy(
            kv.at[own_rows(slot * 8 + detour_to)], legs.at[slot],
            ss.at[slot * 8 + detour_to], legs_r.at[slot],
            device_id={"depth": via}, device_id_type=MESH,
        )

    def second_leg(slot):
        return pltpu.make_async_remote_copy(
            legs.at[slot], kvr.at[between_src], legs_s.at[slot], rs.at[between_src],
            device_id={"depth": slot * 8 + between_dst}, device_id_type=MESH,
        )

    def send_kv(i):
        for j in range(4):
            dest = chunk_of(i) * 4 + j

            in_legs = detour & (dest % 8 == detour_to)

            @pl.when((dest != me) & ~in_legs)
            def _():
                kv_copy(dest, me).start()

            @pl.when(in_legs)
            def _():
                first_leg(dest // 8).start()

    halo = pltpu.make_async_remote_copy(
        kv.at[pl.ds(TOK, WINDOW)], kv.at[pl.ds(0, WINDOW)], halo_s, halo_r,
        device_id={"tok": lax.rem(shard + 1, shards)}, device_id_type=MESH,
    )

    def q_rows(dest):
        return pl.ds(pl.multiple_of(dest * OWN, OWN), OWN)

    def q_direct(dest):
        return pltpu.make_async_remote_copy(
            q.at[q_rows(dest)], qr, qs_sem.at[dest], qr_sem,
            device_id={"depth": dest}, device_id_type=MESH,
        )

    def q_to_relay(dest):
        return pltpu.make_async_remote_copy(
            q.at[q_rows(dest)], relay.at[dest], qs_sem.at[dest], rel_sem.at[dest],
            device_id={"depth": RELAY}, device_id_type=MESH,
        )

    def q_from_relay(dest):
        return pltpu.make_async_remote_copy(
            relay.at[dest], qr, qs_sem.at[dest], qr_sem,
            device_id={"depth": dest}, device_id_type=MESH,
        )

    @pl.when(me != LAST)
    def _():
        load_k.wait()
        load_v.wait()

        def wait_and_project(i, carry):
            load_x(i).wait()
            return project_kv(i, carry)

        lax.fori_loop(0, 4, wait_and_project, 0)
        load_q.start()

    @pl.when(is_last)
    def _():
        load_k.wait()
        load_v.wait()
        load_x(3).wait()
        project_kv(3, 0)
        load_q.wait()
        for i in range(3):
            load_x(i).wait()
        lax.fori_loop(0, 2, project_q_loop, 0)

    pl.semaphore_wait(
        barrier, STEPS - 1 + has_next.astype(jnp.int32) + has_prev.astype(jnp.int32)
    )

    @pl.when(has_next)
    def _():
        halo.start()

    @pl.when(me != LAST)
    def _():
        for i in range(3):
            send_kv(i)
        load_q.wait()
        project_q(0)
        send_kv(3)
        lax.fori_loop(1, 4, project_q_loop, 0)

    @pl.when(is_last)
    def _():
        for dest in RELAYED:
            q_to_relay(dest).start()
        for dest in DIRECT0:
            q_direct(dest).start()
        lax.fori_loop(0, 3, project_kv, 0)
        lax.fori_loop(2, 3, project_q_loop, 0)
        for dest in (11, 10, 9, 8):
            q_direct(dest).start()
        for i in range(4):
            send_kv(i)
        lax.fori_loop(3, 4, project_q_loop, 0)
        qr[...] = q[pl.ds(LAST * OWN, OWN)]

    kvr[me] = kv[own_rows(me)]

    row = lax.broadcasted_iota(jnp.int32, (BQ, KEYS), 0)
    col = lax.broadcasted_iota(jnp.int32, (BQ, KEYS), 1)
    band = (col >= row) & (col <= row + WINDOW)
    bias[0] = jnp.where(band, 0.0, -jnp.inf).astype(F32)
    for b in range(2):
        known = col + (b * BQ - WINDOW) + shard * TOK >= 0
        bias[1 + b] = jnp.where(band & known, 0.0, -jnp.inf).astype(F32)

    def attend(b, edge):
        base = pl.multiple_of(b * BQ, BQ)
        for c in range(HK):
            heads = [
                q[pl.ds(base, BQ), h * HD : (h + 1) * HD] for h in range(c * GROUP, (c + 1) * GROUP)
            ]
            rows = jnp.concatenate(heads, axis=0)
            keys = kv[pl.ds(base, KEYS), c * HD : (c + 1) * HD]
            values = kv[pl.ds(base, KEYS), KW + c * HD : KW + (c + 1) * HD]
            scores = score(rows, keys).reshape(GROUP, BQ, KEYS)
            if edge:
                scores = scores + bias[1 + b][None]
            else:
                scores = jnp.concatenate(
                    [
                        scores[:, :, :BQ] + bias[0, :, :BQ][None],
                        scores[:, :, BQ:WINDOW],
                        scores[:, :, WINDOW:] + bias[0, :, WINDOW:][None],
                    ],
                    axis=-1,
                )
            res = softmax_values(scores.reshape(GROUP * BQ, KEYS), values).astype(BF16)
            for g in range(GROUP):
                h = c * GROUP + g
                out[pl.ds(base, BQ), h * HD : (h + 1) * HD] = res[g * BQ : (g + 1) * BQ]

    def forward(i):
        @pl.when(me == RELAY)
        def _():
            q_to_relay(RELAYED[i]).wait_recv()
            q_from_relay(RELAYED[i]).start()

    for i in range(6):
        attend(i + 2, False)
        if i == 0:

            @pl.when(is_last)
            def _():
                for dest in (12, 13, 14):
                    q_direct(dest).start()

        if i == 1:

            @pl.when(between)
            def _():
                for slot in range(2):
                    first_leg(slot).wait_recv()
                    second_leg(slot).start()

        if i < len(RELAYED):
            forward(i)
    for i in range(6, len(RELAYED)):
        forward(i)

    @pl.when(has_prev)
    def _():
        halo.wait_recv()

    attend(0, True)
    attend(1, True)

    for source in range(STEPS):

        @pl.when(me != source)
        def _():
            kv_copy(source, source).wait_recv()

    @pl.when(me != LAST)
    def _():
        q_direct(LAST).wait_recv()

    for dest in range(STEPS):

        @pl.when(me != dest)
        def _():
            kv_copy(dest, dest).wait_send()

    @pl.when(has_next)
    def _():
        halo.wait_send()

    @pl.when(me == LAST)
    def _():
        for dest in range(LAST):
            q_direct(dest).wait_send()

    @pl.when(me == RELAY)
    def _():
        for dest in RELAYED:
            q_from_relay(dest).wait_send()

    @pl.when(between)
    def _():
        for slot in range(2):
            second_leg(slot).wait_send()


def finish(out, kvr, qr, win_hbm, dep_hbm, dout, sem):
    window = pltpu.make_async_copy(out, win_hbm, sem.at[0])
    window.start()
    token = lax.broadcasted_iota(jnp.int32, (OWN, STEPS * OWN), 0)
    other = lax.broadcasted_iota(jnp.int32, (OWN, STEPS * OWN), 1) % OWN
    for c in range(HK):
        rows = jnp.concatenate(
            [qr[:, h * HD : (h + 1) * HD] for h in range(c * GROUP, (c + 1) * GROUP)], axis=0
        )
        keys = kvr[:, :, c * HD : (c + 1) * HD].reshape(STEPS * OWN, HD)
        values = kvr[:, :, KW + c * HD : KW + (c + 1) * HD].reshape(STEPS * OWN, HD)
        scores = score(rows, keys).reshape(GROUP, OWN, STEPS * OWN)
        scores = jnp.where((token == other)[None], scores, -jnp.inf)
        res = softmax_values(scores.reshape(GROUP * OWN, STEPS * OWN), values).astype(BF16)
        for g in range(GROUP):
            h = c * GROUP + g
            dout[:, h * HD : (h + 1) * HD] = res[g * OWN : (g + 1) * OWN]

    last = pltpu.make_async_copy(dout, dep_hbm, sem.at[1])
    last.start()
    window.wait()
    last.wait()


def body(states, w_query, w_key, w_value):
    any_spec = pl.BlockSpec(memory_space=pltpu.HBM)
    dma = pltpu.SemaphoreType.DMA
    args = [
        pltpu.with_memory_space_constraint(a, pltpu.HBM)
        for a in (states[0], w_query, w_key, w_value)
    ]
    vmem = pl.BlockSpec(memory_space=pltpu.VMEM)
    local = pl.pallas_call(
        kernel,
        out_shape=(
            jax.ShapeDtypeStruct((TOK, QW), BF16),
            jax.ShapeDtypeStruct((STEPS, OWN, 2 * KW), BF16),
            jax.ShapeDtypeStruct((OWN, QW), BF16),
        ),
        in_specs=[any_spec] * 4,
        out_specs=(vmem, vmem, vmem),
        scratch_shapes=[
            pltpu.VMEM((TOK, D), BF16),
            pltpu.VMEM((D, QW), BF16),
            pltpu.VMEM((D, 2 * KW), BF16),
            pltpu.VMEM((TOK, QW), BF16),
            pltpu.VMEM((WINDOW + TOK, 2 * KW), BF16),
            pltpu.VMEM((RELAY, OWN, QW), BF16),
            pltpu.VMEM((2, OWN, 2 * KW), BF16),
            pltpu.VMEM((3, BQ, KEYS), F32),
            dma((7,)),
            dma((STEPS,)),
            dma((STEPS,)),
            dma((2,)),
            dma((2,)),
            dma((STEPS,)),
            dma(()),
            dma((RELAY,)),
            dma(()),
            dma(()),
        ],
        compiler_params=pltpu.CompilerParams(
            collective_id=0, has_side_effects=True, vmem_limit_bytes=40 * 1024 * 1024
        ),
        name="looped_attention",
    )(*args)
    window_out, depth_out = pl.pallas_call(
        finish,
        out_shape=(
            jax.ShapeDtypeStruct((TOK, QW), BF16),
            jax.ShapeDtypeStruct((OWN, QW), BF16),
        ),
        in_specs=[vmem] * 3,
        out_specs=(any_spec, any_spec),
        scratch_shapes=[pltpu.VMEM((OWN, QW), BF16), dma((2,))],
        compiler_params=pltpu.CompilerParams(vmem_limit_bytes=16 * 1024 * 1024),
        name="final_attention",
    )(*local)
    return (window_out[None], depth_out)


def solution(mesh):
    in_specs = (P("depth", "tok", None), P(), P(), P())
    out_specs = (P("depth", "tok", None), P(("tok", "depth"), None))
    return jax.shard_map(body, mesh=mesh, in_specs=in_specs, out_specs=out_specs, check_vma=False)
```

time: 52.2 us -> 45.8 us (0.88)
  local copies, waits for them, and re-layouts: 3.77 us -> 0 us
  Pallas kernels: 47.7 us -> 44.9 us
    pallas_call x1, Pallas kernels: 47.7 us -> 43 us  [body(): pl.pallas_call(kernel, out_shape=(jax.ShapeDtypeStruct((TOK, QW), BF16),...]
    unnamed x4 -> x0, local copies, waits for them, and re-layouts: 3.77 us -> none
    pallas_call x0 -> x1, Pallas kernels: none -> 1.85 us  [body(): pl.pallas_call(finish, out_shape=(jax.ShapeDtypeStruct((TOK, QW), BF16),...]
where the time goes in v2:
time: 45.8 us; the launch traced here: 45.7 us
  Pallas kernels  44.9 us (98%)
  between operations  0.8 us (2%)
    pallas_call x1, Pallas kernels, body(): pl.pallas_call(kernel, out_shape=(jax.ShapeDtypeStruct((TOK, QW), BF16),...  43 us
    pallas_call x1, Pallas kernels, body(): pl.pallas_call(finish, out_shape=(jax.ShapeDtypeStruct((TOK, QW), BF16),...  1.85 us

profile of v2, /device:TPU:217, one launch (start us, length us, event | category | flops | bytes accessed | tf_op | source)
XLA Modules:
  0.0 45.7 jit_solution(7727260189015193801)
XLA Ops:
  0.6 43.0 %looped_attention.1 = (bf16[1024,1024]{1,0:T(8,128)(2,1)S(1)}, bf16[16,64,512]{2,1,0:T(8,128)(2,1)S(1)}, bf16[64,1024]{1,0:T(8,128)(2,1)S(1)}) custom-call(bf16[1024,2048]{1,0:T(8,128)(2,1)} %bitcast.2, bf16[2048,1024]{1,0:T(8,128)(2,1)} %wq_hbm.1, bf16[2048,256]{1,0:T(8,128)(2,1)} %wk_hbm.1, bf16[2048,256]{1,0:T(8,128)(2,1)} %wv_hbm.1), custom_call_target="tpu_custom_call" | custom-call | tf_op jit(solution)/shard_map/looped_attention/pallas_call | solution.py:387
  43.7 1.8 %final_attention.1 = (bf16[1024,1024]{1,0:T(8,128)(2,1)}, bf16[64,1024]{1,0:T(8,128)(2,1)}) custom-call(bf16[1024,1024]{1,0:T(8,128)(2,1)S(1)} %get-tuple-element.7.out, bf16[16,64,512]{2,1,0:T(8,128)(2,1)S(1)} %get-tuple-element.8.kvr, bf16[64,1024]{1,0:T(8,128)(2,1)S(1)} %get-tuple-element.9.qr), custom_call_target="tpu_custom_call" | custom-call | tf_op jit(solution)/shard_map/final_attention/pallas_call | solution.py:421

commit v3 on v2

--- a/solution.py
+++ b/solution.py
@@ -22,8 +22,8 @@
 BQ = 128
 KEYS = BQ + WINDOW
 RELAY = 7
-RELAYED = (3, 2, 4, 1, 5, 6)
-DIRECT0 = (0, 7)
+RELAYED = (0, 2, 1, 3, 4, 5, 6)
+SIDE = (0, 1, 5, 6)
 LAST = STEPS - 1
 SCALE = math.log2(math.e) / math.sqrt(HD)
 MESH = pl.DeviceIdType.MESH
@@ -71,20 +71,10 @@
     load_q = pltpu.make_async_copy(wq_hbm, wq, ld.at[6])
     is_last = me == LAST
 
-    @pl.when(is_last)
-    def _():
-        load_k.start()
-        load_v.start()
-        for i in (3, 0, 2, 1):
-            load_x(i).start()
-        load_q.start()
-
-    @pl.when(me != LAST)
-    def _():
-        load_k.start()
-        load_v.start()
-        for i in range(4):
-            load_x(i).start()
+    load_k.start()
+    load_v.start()
+    for i in range(4):
+        load_x(i).start()
 
     barrier = pltpu.get_barrier_semaphore()
     for step in range(1, STEPS):
@@ -104,21 +94,16 @@
     def _():
         kv[:WINDOW] = jnp.zeros((WINDOW, 2 * KW), BF16)
 
-    def project_kv(i, carry):
+    def project_kv(i):
         kv[pl.ds(pl.multiple_of(WINDOW + chunk_of(i) * CHUNK, CHUNK), CHUNK)] = jnp.dot(
             x[chunk_rows(i)], wkv[...], preferred_element_type=F32
         ).astype(BF16)
-        return carry
 
     def project_q(i):
         rows = pl.ds(pl.multiple_of(i * CHUNK, CHUNK), CHUNK)
         for n in range(2):
             cols = slice(n * 512, (n + 1) * 512)
             q[rows, cols] = jnp.dot(x[rows], wq[:, cols], preferred_element_type=F32).astype(BF16)
-
-    def project_q_loop(i, carry):
-        project_q(i)
-        return carry
 
     def own_rows(dest):
         return pl.ds(pl.multiple_of(WINDOW + dest * OWN, OWN), OWN)
@@ -150,19 +135,46 @@
             device_id={"depth": slot * 8 + between_dst}, device_id_type=MESH,
         )
 
+    on_side = z == SIDE[0]
+    for s in SIDE[1:]:
+        on_side = on_side | (z == s)
+
+    def side_first():
+        return pltpu.make_async_remote_copy(
+            kv.at[own_rows(RELAY)], legs.at[0], ss.at[RELAY], legs_r.at[0],
+            device_id={"depth": z}, device_id_type=MESH,
+        )
+
+    def side_second():
+        return pltpu.make_async_remote_copy(
+            legs.at[0], kvr.at[8 + z], legs_s.at[0], rs.at[8 + z],
+            device_id={"depth": RELAY}, device_id_type=MESH,
+        )
+
     def send_kv(i):
         for j in range(4):
             dest = chunk_of(i) * 4 + j
 
-            in_legs = detour & (dest % 8 == detour_to)
-
-            @pl.when((dest != me) & ~in_legs)
+            direct = dest != me
+            if j < 2:
+                in_legs = detour & (dest % 8 == detour_to)
+                direct = direct & ~in_legs
+
+                @pl.when(in_legs)
+                def _():
+                    first_leg(dest // 8).start()
+
+            if j == 3:
+                by_side = on_side & (x_lo == 1) & (dest == RELAY)
+                direct = direct & ~by_side
+
+                @pl.when(by_side)
+                def _():
+                    side_first().start()
+
+            @pl.when(direct)
             def _():
                 kv_copy(dest, me).start()
-
-            @pl.when(in_legs)
-            def _():
-                first_leg(dest // 8).start()
 
     halo = pltpu.make_async_remote_copy(
         kv.at[pl.ds(TOK, WINDOW)], kv.at[pl.ds(0, WINDOW)], halo_s, halo_r,
@@ -190,62 +202,71 @@
             device_id={"depth": dest}, device_id_type=MESH,
         )
 
-    @pl.when(me != LAST)
-    def _():
-        load_k.wait()
-        load_v.wait()
-
-        def wait_and_project(i, carry):
-            load_x(i).wait()
-            return project_kv(i, carry)
-
-        lax.fori_loop(0, 4, wait_and_project, 0)
-        load_q.start()
-
-    @pl.when(is_last)
-    def _():
-        load_k.wait()
-        load_v.wait()
-        load_x(3).wait()
-        project_kv(3, 0)
-        load_q.wait()
-        for i in range(3):
-            load_x(i).wait()
-        lax.fori_loop(0, 2, project_q_loop, 0)
-
+    load_k.wait()
+    load_v.wait()
+    load_x(0).wait()
+    project_kv(0)
+    load_x(1).wait()
+    load_q.start()
+    project_kv(1)
     pl.semaphore_wait(
         barrier, STEPS - 1 + has_next.astype(jnp.int32) + has_prev.astype(jnp.int32)
     )
+    send_kv(0)
+    load_x(2).wait()
+    project_kv(2)
+    send_kv(1)
+    load_x(3).wait()
+    project_kv(3)
+    send_kv(2)
 
     @pl.when(has_next)
     def _():
         halo.start()
 
-    @pl.when(me != LAST)
-    def _():
-        for i in range(3):
-            send_kv(i)
-        load_q.wait()
-        project_q(0)
-        send_kv(3)
-        lax.fori_loop(1, 4, project_q_loop, 0)
+    load_q.wait()
+    project_q(0)
+    send_kv(3)
+    project_q(1)
 
     @pl.when(is_last)
     def _():
-        for dest in RELAYED:
+        for dest in (0, 2, 1, 3):
             q_to_relay(dest).start()
-        for dest in DIRECT0:
+
+    project_q(2)
+
+    @pl.when(is_last)
+    def _():
+        for dest in (4, 5, 6):
+            q_to_relay(dest).start()
+        q_direct(RELAY).start()
+
+    project_q(3)
+
+    @pl.when(is_last)
+    def _():
+        for dest in (10, 9, 8, 11):
             q_direct(dest).start()
-        lax.fori_loop(0, 3, project_kv, 0)
-        lax.fori_loop(2, 3, project_q_loop, 0)
-        for dest in (11, 10, 9, 8):
+
+    @pl.when(between)
+    def _():
+        for slot in range(2):
+            first_leg(slot).wait_recv()
+            second_leg(slot).start()
+
+    @pl.when(on_side & (x_lo == 0))
+    def _():
+        side_first().wait_recv()
+        side_second().start()
+
+    kvr[me] = kv[own_rows(me)]
+
+    @pl.when(is_last)
+    def _():
+        for dest in (12, 13, 14):
             q_direct(dest).start()
-        for i in range(4):
-            send_kv(i)
-        lax.fori_loop(3, 4, project_q_loop, 0)
         qr[...] = q[pl.ds(LAST * OWN, OWN)]
-
-    kvr[me] = kv[own_rows(me)]
 
     row = lax.broadcasted_iota(jnp.int32, (BQ, KEYS), 0)
     col = lax.broadcasted_iota(jnp.int32, (BQ, KEYS), 1)
@@ -287,27 +308,10 @@
             q_to_relay(RELAYED[i]).wait_recv()
             q_from_relay(RELAYED[i]).start()
 
+    forward(0)
     for i in range(6):
         attend(i + 2, False)
-        if i == 0:
-
-            @pl.when(is_last)
-            def _():
-                for dest in (12, 13, 14):
-                    q_direct(dest).start()
-
-        if i == 1:
-
-            @pl.when(between)
-            def _():
-                for slot in range(2):
-                    first_leg(slot).wait_recv()
-                    second_leg(slot).start()
-
-        if i < len(RELAYED):
-            forward(i)
-    for i in range(6, len(RELAYED)):
-        forward(i)
+        forward(i + 1)
 
     @pl.when(has_prev)
     def _():
@@ -351,10 +355,19 @@
         for slot in range(2):
             second_leg(slot).wait_send()
 
+    @pl.when(on_side & (x_lo == 0))
+    def _():
+        side_second().wait_send()
+
 
 def finish(out, kvr, qr, win_hbm, dep_hbm, dout, sem):
     window = pltpu.make_async_copy(out, win_hbm, sem.at[0])
     window.start()
+
+    def half(c):
+        cols = slice(c * GROUP * HD, (c + 1) * GROUP * HD)
+        return pltpu.make_async_copy(dout.at[:, cols], dep_hbm.at[:, cols], sem.at[1 + c])
+
     token = lax.broadcasted_iota(jnp.int32, (OWN, STEPS * OWN), 0)
     other = lax.broadcasted_iota(jnp.int32, (OWN, STEPS * OWN), 1) % OWN
     for c in range(HK):
@@ -369,11 +382,11 @@
         for g in range(GROUP):
             h = c * GROUP + g
             dout[:, h * HD : (h + 1) * HD] = res[g * OWN : (g + 1) * OWN]
-
-    last = pltpu.make_async_copy(dout, dep_hbm, sem.at[1])
-    last.start()
+        half(c).start()
+
     window.wait()
-    last.wait()
+    for c in range(HK):
+        half(c).wait()
 
 
 def body(states, w_query, w_key, w_value):
@@ -426,7 +439,7 @@
         ),
         in_specs=[vmem] * 3,
         out_specs=(any_spec, any_spec),
-        scratch_shapes=[pltpu.VMEM((OWN, QW), BF16), dma((2,))],
+        scratch_shapes=[pltpu.VMEM((OWN, QW), BF16), dma((3,))],
         compiler_params=pltpu.CompilerParams(vmem_limit_bytes=16 * 1024 * 1024),
         name="final_attention",
     )(*local)

time: 45.8 us -> 43.4 us (0.948)
  Pallas kernels: 44.9 us -> 42.1 us
    pallas_call x1, Pallas kernels: 43 us -> 40.3 us  [body(): pl.pallas_call(kernel, out_shape=(jax.ShapeDtypeStruct((TOK, QW), BF16),...]
where the time goes in v3:
time: 43.4 us; the launch traced here: 42.9 us
  Pallas kernels  42.1 us (97%)
  between operations  0.8 us (2%)
    pallas_call x1, Pallas kernels, body(): pl.pallas_call(kernel, out_shape=(jax.ShapeDtypeStruct((TOK, QW), BF16),...  40.3 us
    pallas_call x1, Pallas kernels, body(): pl.pallas_call(finish, out_shape=(jax.ShapeDtypeStruct((TOK, QW), BF16),...  1.83 us

profile of v3, /device:TPU:217, one launch (start us, length us, event | category | flops | bytes accessed | tf_op | source)
XLA Modules:
  0.0 42.9 jit_solution(10578050962719091661)
XLA Ops:
  0.6 40.3 %looped_attention.1 = (bf16[1024,1024]{1,0:T(8,128)(2,1)S(1)}, bf16[16,64,512]{2,1,0:T(8,128)(2,1)S(1)}, bf16[64,1024]{1,0:T(8,128)(2,1)S(1)}) custom-call(bf16[1024,2048]{1,0:T(8,128)(2,1)} %bitcast.2, bf16[2048,1024]{1,0:T(8,128)(2,1)} %wq_hbm.1, bf16[2048,256]{1,0:T(8,128)(2,1)} %wk_hbm.1, bf16[2048,256]{1,0:T(8,128)(2,1)} %wv_hbm.1), custom_call_target="tpu_custom_call" | custom-call | tf_op jit(solution)/shard_map/looped_attention/pallas_call | solution.py:400
  40.9 1.8 %final_attention.1 = (bf16[1024,1024]{1,0:T(8,128)(2,1)}, bf16[64,1024]{1,0:T(8,128)(2,1)}) custom-call(bf16[1024,1024]{1,0:T(8,128)(2,1)S(1)} %get-tuple-element.7.out, bf16[16,64,512]{2,1,0:T(8,128)(2,1)S(1)} %get-tuple-element.8.kvr, bf16[64,1024]{1,0:T(8,128)(2,1)S(1)} %get-tuple-element.9.qr), custom_call_target="tpu_custom_call" | custom-call | tf_op jit(solution)/shard_map/final_attention/pallas_call | solution.py:434

commit v4 on v3

--- a/solution.py
+++ b/solution.py
@@ -24,6 +24,7 @@
 RELAY = 7
 RELAYED = (0, 2, 1, 3, 4, 5, 6)
 SIDE = (0, 1, 5, 6)
+LEGS_AT = 2
 LAST = STEPS - 1
 SCALE = math.log2(math.e) / math.sqrt(HD)
 MESH = pl.DeviceIdType.MESH
@@ -220,7 +221,9 @@
     project_kv(3)
     send_kv(2)
 
-    @pl.when(has_next)
+    late_halo = is_last & (shard == shards // 2 - 1)
+
+    @pl.when(has_next & ~late_halo)
     def _():
         halo.start()
 
@@ -240,6 +243,11 @@
     def _():
         for dest in (4, 5, 6):
             q_to_relay(dest).start()
+
+        @pl.when(late_halo)
+        def _():
+            halo.start()
+
         q_direct(RELAY).start()
 
     project_q(3)
@@ -248,17 +256,6 @@
     def _():
         for dest in (10, 9, 8, 11):
             q_direct(dest).start()
-
-    @pl.when(between)
-    def _():
-        for slot in range(2):
-            first_leg(slot).wait_recv()
-            second_leg(slot).start()
-
-    @pl.when(on_side & (x_lo == 0))
-    def _():
-        side_first().wait_recv()
-        side_second().start()
 
     kvr[me] = kv[own_rows(me)]
 
@@ -311,6 +308,19 @@
     forward(0)
     for i in range(6):
         attend(i + 2, False)
+        if i == LEGS_AT:
+
+            @pl.when(between)
+            def _():
+                for slot in range(2):
+                    first_leg(slot).wait_recv()
+                    second_leg(slot).start()
+
+            @pl.when(on_side & (x_lo == 0))
+            def _():
+                side_first().wait_recv()
+                side_second().start()
+
         forward(i + 1)
 
     @pl.when(has_prev)

time: 43.4 us -> 44 us (1.014)
  the two profiles are of different devices: /device:TPU:217 before, /device:TPU:230 now
where the time goes in v4:
time: 44 us; the launch traced here: 43.8 us
  Pallas kernels  43 us (98%)
  between operations  0.8 us (2%)
    pallas_call x1, Pallas kernels, body(): pl.pallas_call(kernel, out_shape=(jax.ShapeDtypeStruct((TOK, QW), BF16),...  41.2 us
    pallas_call x1, Pallas kernels, body(): pl.pallas_call(finish, out_shape=(jax.ShapeDtypeStruct((TOK, QW), BF16),...  1.83 us

profile of v4, /device:TPU:230, one launch (start us, length us, event | category | flops | bytes accessed | tf_op | source)
XLA Modules:
  0.0 43.8 jit_solution(15914016529187281820)
XLA Ops:
  0.6 41.2 %looped_attention.1 = (bf16[1024,1024]{1,0:T(8,128)(2,1)S(1)}, bf16[16,64,512]{2,1,0:T(8,128)(2,1)S(1)}, bf16[64,1024]{1,0:T(8,128)(2,1)S(1)}) custom-call(bf16[1024,2048]{1,0:T(8,128)(2,1)} %bitcast.2, bf16[2048,1024]{1,0:T(8,128)(2,1)} %wq_hbm.1, bf16[2048,256]{1,0:T(8,128)(2,1)} %wk_hbm.1, bf16[2048,256]{1,0:T(8,128)(2,1)} %wv_hbm.1), custom_call_target="tpu_custom_call" | custom-call | tf_op jit(solution)/shard_map/looped_attention/pallas_call | solution.py:410
  41.9 1.8 %final_attention.1 = (bf16[1024,1024]{1,0:T(8,128)(2,1)}, bf16[64,1024]{1,0:T(8,128)(2,1)}) custom-call(bf16[1024,1024]{1,0:T(8,128)(2,1)S(1)} %get-tuple-element.7.out, bf16[16,64,512]{2,1,0:T(8,128)(2,1)S(1)} %get-tuple-element.8.kvr, bf16[64,1024]{1,0:T(8,128)(2,1)S(1)} %get-tuple-element.9.qr), custom_call_target="tpu_custom_call" | custom-call | tf_op jit(solution)/shard_map/final_attention/pallas_call | solution.py:444
